TPU v7x, 32 devices: a whole 2x2x4 slice. The times are simulated.
32 devices in a mesh: tm: 2 (over x), height: 4 (over z), head: 4 (over y, core).
Axes of the slice: x: 2, y: 2, z: 4, core: 2. Of those that a mesh axis runs over, the one named last changes fastest.
Arguments:
- query_in: bfloat16 [12, 8, 32, 16, 128], P('head', 'tm', 'height'), may hold values from -8 to 8
- key_in: bfloat16 [12, 8, 32, 16, 128], P('head', 'tm', 'height'), may hold values from -8 to 8
- value_in: bfloat16 [12, 8, 32, 16, 128], P('head', 'tm', 'height'), may hold values from -6 to 6
- out_grad: bfloat16 [12, 8, 32, 16, 128], P('head', 'tm', 'height'), may hold values from -6 to 6
Outputs:
- query_grad: bfloat16 [12, 8, 32, 16, 128], P('head', 'tm', 'height')
- key_grad: bfloat16 [12, 8, 32, 16, 128], P('head', 'tm', 'height')
- value_grad: bfloat16 [12, 8, 32, 16, 128], P('head', 'tm', 'height')
All inputs are finite; a program needn't handle non-finite values.
Results may differ from a plain program's by a relative error of at most 0.0093.
Values may be sent and summed in bfloat16 or wider, within the bound.
A program may use at most 128 MiB of HBM per device.

v0:
```python
import jax
import jax.numpy as jnp
from jax import lax
from jax.sharding import PartitionSpec as P

TILE_C = 8


def shifted(block, axis, distance):
    devices = range(lax.axis_size(axis))
    route = [(i - distance, i) for i in devices if i - distance in devices]
    return lax.ppermute(block, axis, route)


def shortened(x):
    return jax.tree.map(lambda a: a.astype(jnp.bfloat16) if a.dtype == jnp.float32 else a, x)


def extended(x, sides, width):
    for axis, dim in sides:
        size, length = (lax.axis_size(axis), x.shape[dim])
        up = [(i, (i + 1) % size) for i in range(size - 1)]
        down = [(j, i) for i, j in up]
        last = lax.slice_in_dim(x, length - width, length, axis=dim)
        first = lax.slice_in_dim(x, 0, width, axis=dim)
        before = lax.ppermute(last, axis, up)
        after = lax.ppermute(first, axis, down)
        x = jnp.concatenate([before, x, after], axis=dim)
    return x


def neighbour_live():
    offsets = jnp.arange(3, dtype=jnp.int32) - 1
    frame_pos = lax.axis_index("tm") + offsets
    row_pos = lax.axis_index("height") + offsets
    frame_ok = (frame_pos >= 0) & (frame_pos < lax.axis_size("tm"))
    row_ok = (row_pos >= 0) & (row_pos < lax.axis_size("height"))
    return frame_ok[:, None] & row_ok[None, :]


def span_live(neighbour_ok, tile_index, span_start, frame_count, row_count, span_width, col_tile):
    columns = span_start + jnp.arange(span_width, dtype=jnp.int32)
    near_cols = jnp.abs(columns // col_tile - tile_index) <= 1
    live_mask = neighbour_ok[:, :, None, None, None] & near_cols[None, None, None, None, :]
    return jnp.broadcast_to(live_mask, (3, 3, frame_count, row_count, span_width)).reshape(-1)


def scores_of(left_rows, right_rows, live_mask, score_scale):
    raw_scores = (
        jnp.einsum("hqd,hkd->hqk", left_rows, right_rows, preferred_element_type=jnp.float32)
        * score_scale
    )
    return jnp.where(live_mask, raw_scores, -jnp.inf)


def whole_span(array, span_start, span_size, axis_pos):
    return isinstance(span_start, int) and span_start == 0 and (span_size == array.shape[axis_pos])


def cut_span(array, span_start, span_size, axis_pos):
    if whole_span(array, span_start, span_size, axis_pos):
        return array
    return lax.dynamic_slice_in_dim(array, jnp.asarray(span_start, jnp.int32), span_size, axis_pos)


def add_span(array, piece):
    return array + piece


def run_tiles(tile_step, tile_count, col_tile, carried):
    edge_width = 2 * col_tile
    carried = tile_step(0, 0, edge_width, carried)
    return tile_step(tile_count - 1, (tile_count - 2) * col_tile, edge_width, carried)


def send_rows(parts, offset):
    return (
        shifted(parts[0].astype(jnp.bfloat16), "height", offset).astype(jnp.float32),
        shifted(parts[1].astype(jnp.bfloat16), "height", offset).astype(jnp.float32),
    )


def send_frames(parts, offset):
    return shifted((shortened(parts[0]), shortened(parts[1])), "tm", offset)


def local(query_in, key_in, value_in, out_grad):
    head_count, frame_count, row_count, col_count, head_depth = query_in.shape
    col_tile = TILE_C
    tile_count = col_count // col_tile
    score_scale = head_depth ** (-0.5)
    spread_shape = (head_count, 1, 1, frame_count, row_count, col_count, head_depth)
    ext_shape = (head_count, 3, 3, frame_count, row_count, col_count, head_depth)
    stat_shape = (head_count, frame_count, row_count, col_tile)
    neighbour_ok = neighbour_live()
    keys_ext, values_ext = (
        extended(key_in.reshape(spread_shape), (("tm", 1), ("height", 2)), 1),
        extended(value_in.reshape(spread_shape), (("tm", 1), ("height", 2)), 1),
    )

    def query_step(tile_index, span_start, span_width, carried):
        grad_q, row_totals, row_deltas, grad_k, grad_v = carried
        own_start = jnp.asarray(tile_index * col_tile, jnp.int32)
        q_rows = cut_span(query_in, own_start, col_tile, 3).reshape(head_count, -1, head_depth)
        g_rows = cut_span(out_grad, own_start, col_tile, 3).reshape(head_count, -1, head_depth)
        k_span = cut_span(keys_ext, span_start, span_width, 5).reshape(head_count, -1, head_depth)
        v_span = cut_span(values_ext, span_start, span_width, 5).reshape(head_count, -1, head_depth)
        live_mask = span_live(
            neighbour_ok, tile_index, span_start, frame_count, row_count, span_width, col_tile
        )
        scores = scores_of(q_rows, k_span, live_mask[None, None, :], score_scale)
        row_max = jnp.max(scores, axis=-1, keepdims=True)
        log_total = row_max + jnp.log(jnp.sum(jnp.exp(scores - row_max), axis=-1, keepdims=True))
        weights = jnp.exp(scores - log_total)
        weight_bf = weights.astype(jnp.bfloat16)
        attended = jnp.einsum("hqk,hkd->hqd", weight_bf, v_span, preferred_element_type=jnp.float32)
        row_delta = jnp.sum(g_rows.astype(jnp.float32) * attended, axis=-1, keepdims=True)
        d_weights = jnp.einsum("hqd,hkd->hqk", g_rows, v_span, preferred_element_type=jnp.float32)
        d_scores = (weights * (d_weights - row_delta)).astype(jnp.bfloat16)
        grad_piece = (
            jnp.einsum("hqk,hkd->hqd", d_scores, k_span, preferred_element_type=jnp.float32)
            * score_scale
        )
        grad_q = lax.dynamic_update_slice_in_dim(
            grad_q, grad_piece.reshape(stat_shape + (head_depth,)), own_start, 3
        )
        row_totals = lax.dynamic_update_slice_in_dim(
            row_totals, log_total.reshape(stat_shape), own_start, 3
        )
        row_deltas = lax.dynamic_update_slice_in_dim(
            row_deltas, row_delta.reshape(stat_shape), own_start, 3
        )
        span_shape = (head_count, 3, 3, frame_count, row_count, span_width, head_depth)
        key_piece = (
            jnp.einsum("hqk,hqd->hkd", d_scores, q_rows, preferred_element_type=jnp.float32)
            * score_scale
        )
        value_piece = jnp.einsum(
            "hqk,hqd->hkd", weight_bf, g_rows, preferred_element_type=jnp.float32
        )
        grad_k = add_span(grad_k, key_piece.reshape(span_shape))
        grad_v = add_span(grad_v, value_piece.reshape(span_shape))
        return (grad_q, row_totals, row_deltas, grad_k, grad_v)

    stat_full = (head_count, frame_count, row_count, col_count)
    initial = (
        jnp.zeros(query_in.shape, jnp.float32),
        jnp.zeros(stat_full, jnp.float32),
        jnp.zeros(stat_full, jnp.float32),
        jnp.zeros(ext_shape, jnp.float32),
        jnp.zeros(ext_shape, jnp.float32),
    )
    grad_q, row_totals, row_deltas, grad_k, grad_v = run_tiles(
        query_step, tile_count, col_tile, initial
    )
    query_grad = grad_q.astype(jnp.bfloat16)
    from_above = send_rows((grad_k[:, :, 0], grad_v[:, :, 0]), -1)
    from_below = send_rows((grad_k[:, :, 2], grad_v[:, :, 2]), 1)
    part_k = grad_k[:, :, 1] + from_above[0] + from_below[0]
    part_v = grad_v[:, :, 1] + from_above[1] + from_below[1]
    from_next = send_frames((part_k[:, 0], part_v[:, 0]), -1)
    from_prev = send_frames((part_k[:, 2], part_v[:, 2]), 1)
    key_total = part_k[:, 1] + from_next[0] + from_prev[0]
    value_total = part_v[:, 1] + from_next[1] + from_prev[1]
    return (query_grad, key_total.astype(jnp.bfloat16), value_total.astype(jnp.bfloat16))


def solution(mesh):
    return jax.shard_map(
        local,
        mesh=mesh,
        in_specs=(
            P("head", "tm", "height", None, None),
            P("head", "tm", "height", None, None),
            P("head", "tm", "height", None, None),
            P("head", "tm", "height", None, None),
        ),
        out_specs=(
            P("head", "tm", "height", None, None),
            P("head", "tm", "height", None, None),
            P("head", "tm", "height", None, None),
        ),
        check_vma=False,
    )
```

profile of v0, /device:TPU:10, one launch (start us, length us, event | category | flops | bytes accessed | tf_op | source)
XLA Modules:
  0.0 207.7 jit_solution(3280205000205700873)
XLA Ops:
  2.1 4.6 %collective-permute-start.1 = (bf16[3,1,1,4,8,16,128]{6,5,4,3,0,2,1:T(8,128)(2,1)}, bf16[3,1,1,4,8,16,128]{6,5,4,3,0,2,1:T(8,128)(2,1)S(1)}, u32[]{:S(2)}, u32[]{:S(2)}) collective-permute-start(bf16[3,1,1,4,8,16,128]{6,5,4,3,0,2,1:T(8,128)(2,1)} %bitcast.155), channel_id=1, source_target_pairs={{16,0},{17,1},{18,2},{19,3},{20,4},{21,5},{22,6},{23,7},{24,8},{25... | collective-permute-start | bytes 1179656 | tf_op jit(solution)/shard_map/ppermute | solution.py:27
  8.0 4.6 %collective-permute-start.5 = (bf16[3,1,1,4,8,16,128]{6,5,4,3,0,2,1:T(8,128)(2,1)}, bf16[3,1,1,4,8,16,128]{6,5,4,3,0,2,1:T(8,128)(2,1)S(1)}, u32[]{:S(2)}, u32[]{:S(2)}) collective-permute-start(bf16[3,1,1,4,8,16,128]{6,5,4,3,0,2,1:T(8,128)(2,1)} %bitcast.159), channel_id=1, source_target_pairs={{16,0},{17,1},{18,2},{19,3},{20,4},{21,5},{22,6},{23,7},{24,8},{25... | collective-permute-start | bytes 1179656 | tf_op jit(solution)/shard_map/ppermute | solution.py:27
  18.6 3.5 %collective-permute-start.2 = (bf16[3,3,1,4,8,16,128]{6,5,4,3,0,2,1:T(8,128)(2,1)}, bf16[3,3,1,4,8,16,128]{6,5,4,3,0,2,1:T(8,128)(2,1)}, u32[]{:S(2)}, u32[]{:S(2)}) collective-permute-start(bf16[3,3,1,4,8,16,128]{6,5,4,3,0,2,1:T(8,128)(2,1)} %pad_maximum_fusion.2), channel_id=1, source_target_pairs={{0,4},{4,8},{8,12},{1,5},{5,9},{9,13},{2,6},{6,10},{10,14},{3,7},{... | collective-permute-start | bytes 3538952 | tf_op jit(solution)/shard_map/ppermute | solution.py:26
  22.1 3.3 %collective-permute-start.3 = (bf16[3,3,1,4,8,16,128]{6,5,4,3,0,2,1:T(8,128)(2,1)}, bf16[3,3,1,4,8,16,128]{6,5,4,3,0,2,1:T(8,128)(2,1)}, u32[]{:S(2)}, u32[]{:S(2)}) collective-permute-start(bf16[3,3,1,4,8,16,128]{6,5,4,3,0,2,1:T(8,128)(2,1)} %pad_maximum_fusion.2), channel_id=1, source_target_pairs={{4,0},{8,4},{12,8},{5,1},{9,5},{13,9},{6,2},{10,6},{14,10},{7,3},{... | collective-permute-start | bytes 3538952 | tf_op jit(solution)/shard_map/ppermute | solution.py:27
  31.6 4.3 %collective-permute-start.7 = (bf16[3,3,1,4,8,16,128]{6,5,4,3,0,2,1:T(8,128)(2,1)}, bf16[3,3,1,4,8,16,128]{6,5,4,3,0,2,1:T(8,128)(2,1)}, u32[]{:S(2)}, u32[]{:S(2)}) collective-permute-start(bf16[3,3,1,4,8,16,128]{6,5,4,3,0,2,1:T(8,128)(2,1)} %pad_maximum_fusion.3), channel_id=1, source_target_pairs={{4,0},{8,4},{12,8},{5,1},{9,5},{13,9},{6,2},{10,6},{14,10},{7,3},{... | collective-permute-start | bytes 3538952 | tf_op jit(solution)/shard_map/ppermute | solution.py:27
  36.0 13.7 %collective-permute-done.2 = bf16[3,3,1,4,8,16,128]{6,5,4,3,0,2,1:T(8,128)(2,1)} collective-permute-done((bf16[3,3,1,4,8,16,128]{6,5,4,3,0,2,1:T(8,128)(2,1)}, bf16[3,3,1,4,8,16,128]{6,5,4,3,0,2,1:T(8,128)(2,1)}, u32[]{:S(2)}, u32[]{:S(2)}) %collective-permute-start.2) | collective-permute-done | bytes 1179680 | tf_op jit(solution)/shard_map/ppermute | solution.py:26
  49.7 3.5 %collective-permute-done.3 = bf16[3,3,1,4,8,16,128]{6,5,4,3,0,2,1:T(8,128)(2,1)} collective-permute-done((bf16[3,3,1,4,8,16,128]{6,5,4,3,0,2,1:T(8,128)(2,1)}, bf16[3,3,1,4,8,16,128]{6,5,4,3,0,2,1:T(8,128)(2,1)}, u32[]{:S(2)}, u32[]{:S(2)}) %collective-permute-start.3) | collective-permute-done | bytes 1179680 | tf_op jit(solution)/shard_map/ppermute | solution.py:27
  56.3 4.3 %bitcast_reduce_fusion.1 = (f32[3,256]{1,0:T(4,128)S(1)}, f32[3,4608,256]{2,1,0:T(8,128)S(1)}) fusion(bf16[3,4608,128]{2,1,0:T(8,128)(2,1)S(1)} %bitcast.134, bf16[3,256,128]{2,1,0:T(8,128)(2,1)S(1)} %bitcast.152, pred[4608]{0:T(1024)(128)(4,1)S(1)} %broadcast_in_dim.46), kind=kOutput, calls=%fused_computation.12 | convolution fusion | flops 916585728 | bytes 17899008 | tf_op jit(solution)/shard_map/hqd,hkd->hqk/dot_general | solution.py:50
  62.4 9.7 %bitcast_reduce_fusion = (f32[3,256]{1,0:T(4,128)S(1)}, f32[3,4608,256]{2,1,0:T(8,128)}) fusion(bf16[3,4608,128]{2,1,0:T(8,128)(2,1)} %bitcast.135, bf16[3,256,128]{2,1,0:T(8,128)(2,1)} %bitcast.150, pred[4608]{0:T(1024)(128)(4,1)S(1)} %broadcast_in_dim.50), kind=kOutput, calls=%fused_computation.4 | convolution fusion | flops 916585728 | bytes 17899008 | tf_op jit(solution)/shard_map/hqd,hkd->hqk/dot_general | solution.py:50
  72.1 6.9 %fusion.2 = f32[3,256]{1,0:T(4,128)S(1)} fusion(f32[3,4608,256]{2,1,0:T(8,128)} %get-tuple-element.22, f32[3,256]{1,0:T(4,128)S(1)} %get-tuple-element.21), kind=kLoop, calls=%fused_computation.6 | loop fusion | flops 7077120 | bytes 14161920 | tf_op jit(solution)/shard_map/reduce_sum | solution.py:113
  84.2 4.9 %fusion.18 = f32[3,4608,128]{2,1,0:T(8,128)} fusion(bf16[3,256,128]{2,1,0:T(8,128)(2,1)S(1)} %bitcast.147, f32[3,4608,256]{2,1,0:T(8,128)S(1)} %get-tuple-element.24, f32[3,256]{1,0:T(4,128)S(1)} %log_add_fusion.1), kind=kOutput, calls=%fused_computation.32 | convolution fusion | flops 913047552 | bytes 21433344 | tf_op jit(solution)/shard_map/hqk,hqd->hkd/dot_general | solution.py:138
  89.0 9.3 %fusion.33 = f32[3,256]{1,0:T(4,128)S(1)} fusion(bf16[3,4608,128]{2,1,0:T(8,128)(2,1)} %bitcast.130, f32[3,4608,256]{2,1,0:T(8,128)} %copy-done, f32[3,256]{1,0:T(4,128)S(1)} %log_add_fusion.1, bf16[3,256,128]{2,1,0:T(8,128)(2,1)S(1)} %bitcast.148), kind=kOutput, calls=%fused_computation.47 | convolution fusion | flops 913341696 | bytes 17897472 | tf_op jit(solution)/shard_map/hqk,hkd->hqd/dot_general | solution.py:116
  98.4 8.3 %fusion.30 = f32[3,256]{1,0:T(4,128)S(1)} fusion(bf16[3,4608,128]{2,1,0:T(8,128)(2,1)S(1)} %bitcast.131, f32[3,4608,256]{2,1,0:T(8,128)} %get-tuple-element.22, f32[3,256]{1,0:T(4,128)S(1)} %log_add_fusion, bf16[3,256,128]{2,1,0:T(8,128)(2,1)S(1)} %bitcast.144), kind=kOutput, calls=%fused_computation.46 | convolution fusion | flops 913341696 | bytes 17897472 | tf_op jit(solution)/shard_map/hqk,hkd->hqd/dot_general | solution.py:116
  106.6 12.0 %convolution_add_fusion = f32[3,4608,128]{2,1,0:T(8,128)} fusion(f32[3,4608,128]{2,1,0:T(8,128)} %fusion.18, bf16[3,256,128]{2,1,0:T(8,128)(2,1)S(1)} %bitcast.145, f32[3,4608,256]{2,1,0:T(8,128)} %get-tuple-element.22, f32[3,256]{1,0:T(4,128)S(1)} %log_add_fusion), kind=kOutput, calls=%fused_computation.20 | convolution fusion | flops 914817024 | bytes 28511232 | tf_op jit(solution)/shard_map/hqk,hqd->hkd/dot_general | solution.py:138
  118.6 3.8 %slice_bitcast_fusion.3 = (bf16[3,3,4,8,16,128]{5,4,3,2,0,1:T(8,128)(2,1)}, bf16[3,3,4,8,16,128]{5,4,3,2,0,1:T(8,128)(2,1)S(1)}) fusion(f32[3,3,3,4,8,16,128]{6,5,4,3,2,1,0:T(8,128)} %bitcast.140), kind=kLoop, calls=%fused_computation.39 | loop fusion | bytes 4718592 | tf_op jit(solution)/shard_map/convert_element_type | solution.py:79
  128.4 8.6 %fusion.4 = bf16[3,256,4608]{1,2,0:T(8,128)(2,1)} fusion(f32[3,4608,256]{2,1,0:T(8,128)} %copy-done, bf16[3,4608,128]{2,1,0:T(8,128)(2,1)S(1)} %bitcast.132, bf16[3,256,128]{2,1,0:T(8,128)(2,1)S(1)} %bitcast.149, f32[3,256]{1,0:T(4,128)S(1)} %fusion.33, f32[3,256]{1,0:T(4,128)S(1)} %log_add_fusion.1), kind=kOutput, calls=%fused_computation.9 | convolution fusion | flops 920125440 | bytes 24975360 | tf_op jit(solution)/shard_map/hqd,hkd->hqk/dot_general | solution.py:118
  136.9 7.9 %fusion.48 = f32[3,4608,128]{2,1,0:T(8,128)} fusion(bf16[3,256,4608]{1,2,0:T(8,128)(2,1)} %fusion.4, bf16[3,256,128]{2,1,0:T(8,128)(2,1)S(1)} %bitcast.153), kind=kOutput, calls=%fused_computation.81 | convolution fusion | flops 905969664 | bytes 14352384 | tf_op jit(solution)/shard_map/hqk,hqd->hkd/dot_general | solution.py:135
  144.9 8.3 %fusion = bf16[3,256,4608]{1,2,0:T(8,128)(2,1)} fusion(f32[3,4608,256]{2,1,0:T(8,128)} %get-tuple-element.22, bf16[3,4608,128]{2,1,0:T(8,128)(2,1)S(1)} %bitcast.133, bf16[3,256,128]{2,1,0:T(8,128)(2,1)S(1)} %bitcast.146, f32[3,256]{1,0:T(4,128)S(1)} %fusion.30, f32[3,256]{1,0:T(4,128)S(1)} %log_add_fusion), kind=kOutput, calls=%fused_computation.1 | convolution fusion | flops 920125440 | bytes 24975360 | tf_op jit(solution)/shard_map/hqd,hkd->hqk/dot_general | solution.py:118
  153.2 7.2 %fusion.10 = f32[3,4608,128]{2,1,0:T(8,128)S(1)} fusion(f32[3,4608,128]{2,1,0:T(8,128)} %fusion.48, bf16[3,256,4608]{1,2,0:T(8,128)(2,1)} %fusion, bf16[3,256,128]{2,1,0:T(8,128)(2,1)S(1)} %bitcast.151), kind=kOutput, calls=%fused_computation.22 | convolution fusion | flops 909508608 | bytes 21430272 | tf_op jit(solution)/shard_map/hqk,hqd->hkd/dot_general | solution.py:135
  164.4 4.1 %collective-permute-start.8 = (bf16[3,3,4,8,16,128]{5,4,3,2,0,1:T(8,128)(2,1)}, bf16[3,3,4,8,16,128]{5,4,3,2,0,1:T(8,128)(2,1)S(1)}, u32[]{:S(2)}, u32[]{:S(2)}) collective-permute-start(bf16[3,3,4,8,16,128]{5,4,3,2,0,1:T(8,128)(2,1)} %get-tuple-element.9), channel_id=1, source_target_pairs={{4,0},{8,4},{12,8},{5,1},{9,5},{13,9},{6,2},{10,6},{14,10},{7,3},{... | collective-permute-start | bytes 3538952 | tf_op jit(solution)/shard_map/ppermute | solution.py:12
  179.3 4.3 %collective-permute-start.14 = (bf16[3,4,8,16,128]{4,3,2,1,0:T(8,128)(2,1)S(1)}, bf16[3,4,8,16,128]{4,3,2,1,0:T(8,128)(2,1)S(1)}, u32[]{:S(2)}, u32[]{:S(2)}) collective-permute-start(bf16[3,4,8,16,128]{4,3,2,1,0:T(8,128)(2,1)S(1)} %get-tuple-element.11), channel_id=1, source_target_pairs={{16,0},{17,1},{18,2},{19,3},{20,4},{21,5},{22,6},{23,7},{24,8},{25... | collective-permute-start | bytes 1179656 | tf_op jit(solution)/shard_map/ppermute | solution.py:12
  186.0 4.1 %collective-permute-done.9 = bf16[3,3,4,8,16,128]{5,4,3,2,0,1:T(8,128)(2,1)} collective-permute-done((bf16[3,3,4,8,16,128]{5,4,3,2,0,1:T(8,128)(2,1)S(1)}, bf16[3,3,4,8,16,128]{5,4,3,2,0,1:T(8,128)(2,1)}, u32[]{:S(2)}, u32[]{:S(2)}) %collective-permute-start.9) | collective-permute-done | bytes 1179680 | tf_op jit(solution)/shard_map/ppermute | solution.py:12
  192.8 4.3 %collective-permute-start.10 = (bf16[3,4,8,16,128]{4,3,2,1,0:T(8,128)(2,1)S(1)}, bf16[3,4,8,16,128]{4,3,2,1,0:T(8,128)(2,1)S(1)}, u32[]{:S(2)}, u32[]{:S(2)}) collective-permute-start(bf16[3,4,8,16,128]{4,3,2,1,0:T(8,128)(2,1)S(1)} %get-tuple-element.13), channel_id=1, source_target_pairs={{16,0},{17,1},{18,2},{19,3},{20,4},{21,5},{22,6},{23,7},{24,8},{25... | collective-permute-start | bytes 1179656 | tf_op jit(solution)/shard_map/ppermute | solution.py:12
  202.4 4.4 %collective-permute-done.11 = bf16[3,4,8,16,128]{4,3,2,1,0:T(8,128)(2,1)S(1)} collective-permute-done((bf16[3,4,8,16,128]{4,3,2,1,0:T(8,128)(2,1)S(1)}, bf16[3,4,8,16,128]{4,3,2,1,0:T(8,128)(2,1)S(1)}, u32[]{:S(2)}, u32[]{:S(2)}) %collective-permute-start.11) | collective-permute-done | bytes 393248 | tf_op jit(solution)/shard_map/ppermute | solution.py:12
  (82 shorter events, 56.7 us)
Async XLA Ops:
  0.6 52.5 %copy-start.9 = (bf16[3,4,8,16,128]{4,3,2,1,0:T(8,128)(2,1)S(1)}, bf16[3,4,8,16,128]{4,3,2,1,0:T(8,128)(2,1)}, u32[]{:S(2)}) copy-start(bf16[3,4,8,16,128]{4,3,2,1,0:T(8,128)(2,1)} %param.5) | copy-start | bytes 1179652
  0.6 27.2 %copy-start.10 = (bf16[3,4,8,16,128]{4,3,2,1,0:T(8,128)(2,1)S(1)}, bf16[3,4,8,16,128]{4,3,2,1,0:T(8,128)(2,1)}, u32[]{:S(2)}) copy-start(bf16[3,4,8,16,128]{4,3,2,1,0:T(8,128)(2,1)} %param.6) | copy-start | bytes 1179652
  0.7 27.0 %copy-start.13 = (bf16[3,4,8,16,128]{4,3,2,1,0:T(8,128)(2,1)S(1)}, bf16[3,4,8,16,128]{4,3,2,1,0:T(8,128)(2,1)}, u32[]{:S(2)}) copy-start(bf16[3,4,8,16,128]{4,3,2,1,0:T(8,128)(2,1)} %param.7) | copy-start | bytes 1179652
  0.7 14.2 %collective-permute-start = (bf16[3,1,1,4,8,16,128]{6,5,4,3,0,2,1:T(8,128)(2,1)}, bf16[3,1,1,4,8,16,128]{6,5,4,3,0,2,1:T(8,128)(2,1)S(1)}, u32[]{:S(2)}, u32[]{:S(2)}) collective-permute-start(bf16[3,1,1,4,8,16,128]{6,5,4,3,0,2,1:T(8,128)(2,1)} %bitcast.154), channel_id=1, source_target_pairs={{0,16},{1,17},{2,18},{3,19},{4,20},{5,21},{6,22},{7,23},{8,24},{9,... | collective-permute-start | bytes 1179656 | tf_op jit(solution)/shard_map/ppermute | solution.py:26
  2.1 14.4 %collective-permute-start.1 = (bf16[3,1,1,4,8,16,128]{6,5,4,3,0,2,1:T(8,128)(2,1)}, bf16[3,1,1,4,8,16,128]{6,5,4,3,0,2,1:T(8,128)(2,1)S(1)}, u32[]{:S(2)}, u32[]{:S(2)}) collective-permute-start(bf16[3,1,1,4,8,16,128]{6,5,4,3,0,2,1:T(8,128)(2,1)} %bitcast.155), channel_id=1, source_target_pairs={{16,0},{17,1},{18,2},{19,3},{20,4},{21,5},{22,6},{23,7},{24,8},{25... | collective-permute-start | bytes 1179656 | tf_op jit(solution)/shard_map/ppermute | solution.py:27
  6.7 21.1 %collective-permute-start.4 = (bf16[3,1,1,4,8,16,128]{6,5,4,3,0,2,1:T(8,128)(2,1)}, bf16[3,1,1,4,8,16,128]{6,5,4,3,0,2,1:T(8,128)(2,1)S(1)}, u32[]{:S(2)}, u32[]{:S(2)}) collective-permute-start(bf16[3,1,1,4,8,16,128]{6,5,4,3,0,2,1:T(8,128)(2,1)} %bitcast.158), channel_id=1, source_target_pairs={{0,16},{1,17},{2,18},{3,19},{4,20},{5,21},{6,22},{7,23},{8,24},{9,... | collective-permute-start | bytes 1179656 | tf_op jit(solution)/shard_map/ppermute | solution.py:26
  8.0 19.8 %collective-permute-start.5 = (bf16[3,1,1,4,8,16,128]{6,5,4,3,0,2,1:T(8,128)(2,1)}, bf16[3,1,1,4,8,16,128]{6,5,4,3,0,2,1:T(8,128)(2,1)S(1)}, u32[]{:S(2)}, u32[]{:S(2)}) collective-permute-start(bf16[3,1,1,4,8,16,128]{6,5,4,3,0,2,1:T(8,128)(2,1)} %bitcast.159), channel_id=1, source_target_pairs={{16,0},{17,1},{18,2},{19,3},{20,4},{21,5},{22,6},{23,7},{24,8},{25... | collective-permute-start | bytes 1179656 | tf_op jit(solution)/shard_map/ppermute | solution.py:27
  18.6 31.0 %collective-permute-start.2 = (bf16[3,3,1,4,8,16,128]{6,5,4,3,0,2,1:T(8,128)(2,1)}, bf16[3,3,1,4,8,16,128]{6,5,4,3,0,2,1:T(8,128)(2,1)}, u32[]{:S(2)}, u32[]{:S(2)}) collective-permute-start(bf16[3,3,1,4,8,16,128]{6,5,4,3,0,2,1:T(8,128)(2,1)} %pad_maximum_fusion.2), channel_id=1, source_target_pairs={{0,4},{4,8},{8,12},{1,5},{5,9},{9,13},{2,6},{6,10},{10,14},{3,7},{... | collective-permute-start | bytes 3538952 | tf_op jit(solution)/shard_map/ppermute | solution.py:26
  22.1 31.1 %collective-permute-start.3 = (bf16[3,3,1,4,8,16,128]{6,5,4,3,0,2,1:T(8,128)(2,1)}, bf16[3,3,1,4,8,16,128]{6,5,4,3,0,2,1:T(8,128)(2,1)}, u32[]{:S(2)}, u32[]{:S(2)}) collective-permute-start(bf16[3,3,1,4,8,16,128]{6,5,4,3,0,2,1:T(8,128)(2,1)} %pad_maximum_fusion.2), channel_id=1, source_target_pairs={{4,0},{8,4},{12,8},{5,1},{9,5},{13,9},{6,2},{10,6},{14,10},{7,3},{... | collective-permute-start | bytes 3538952 | tf_op jit(solution)/shard_map/ppermute | solution.py:27
  27.7 28.6 %copy-start.7 = (bf16[3,4,8,8,128]{4,3,2,1,0:T(8,128)(2,1)}, bf16[3,4,8,8,128]{4,3,2,1,0:T(8,128)(2,1)S(1)}, u32[]{:S(2)}) copy-start(bf16[3,4,8,8,128]{4,3,2,1,0:T(8,128)(2,1)S(1)} %get-tuple-element.17) | copy-start | bytes 589828
  27.8 27.2 %copy-start.11 = (bf16[3,1,1,4,8,16,128]{6,5,4,3,0,2,1:T(8,128)(2,1)}, bf16[3,1,1,4,8,16,128]{6,5,4,3,0,2,1:T(8,128)(2,1)S(1)}, u32[]{:S(2)}) copy-start(bf16[3,1,1,4,8,16,128]{6,5,4,3,0,2,1:T(8,128)(2,1)S(1)} %collective-permute-done.4) | copy-start | bytes 1179652
  27.8 27.2 %copy-start.12 = (bf16[3,1,1,4,8,16,128]{6,5,4,3,0,2,1:T(8,128)(2,1)}, bf16[3,1,1,4,8,16,128]{6,5,4,3,0,2,1:T(8,128)(2,1)S(1)}, u32[]{:S(2)}) copy-start(bf16[3,1,1,4,8,16,128]{6,5,4,3,0,2,1:T(8,128)(2,1)S(1)} %collective-permute-done.5) | copy-start | bytes 1179652
  29.1 49.9 %collective-permute-start.6 = (bf16[3,3,1,4,8,16,128]{6,5,4,3,0,2,1:T(8,128)(2,1)}, bf16[3,3,1,4,8,16,128]{6,5,4,3,0,2,1:T(8,128)(2,1)}, u32[]{:S(2)}, u32[]{:S(2)}) collective-permute-start(bf16[3,3,1,4,8,16,128]{6,5,4,3,0,2,1:T(8,128)(2,1)} %pad_maximum_fusion.3), channel_id=1, source_target_pairs={{0,4},{4,8},{8,12},{1,5},{5,9},{9,13},{2,6},{6,10},{10,14},{3,7},{... | collective-permute-start | bytes 3538952 | tf_op jit(solution)/shard_map/ppermute | solution.py:26
  31.6 47.4 %collective-permute-start.7 = (bf16[3,3,1,4,8,16,128]{6,5,4,3,0,2,1:T(8,128)(2,1)}, bf16[3,3,1,4,8,16,128]{6,5,4,3,0,2,1:T(8,128)(2,1)}, u32[]{:S(2)}, u32[]{:S(2)}) collective-permute-start(bf16[3,3,1,4,8,16,128]{6,5,4,3,0,2,1:T(8,128)(2,1)} %pad_maximum_fusion.3), channel_id=1, source_target_pairs={{4,0},{8,4},{12,8},{5,1},{9,5},{13,9},{6,2},{10,6},{14,10},{7,3},{... | collective-permute-start | bytes 3538952 | tf_op jit(solution)/shard_map/ppermute | solution.py:27
  60.6 23.6 %copy-start = (f32[3,4608,256]{2,1,0:T(8,128)}, f32[3,4608,256]{2,1,0:T(8,128)S(1)}, u32[]{:S(2)}) copy-start(f32[3,4608,256]{2,1,0:T(8,128)S(1)} %get-tuple-element.24) | copy-start | bytes 42467332
  122.4 54.1 %collective-permute-start.12 = (bf16[3,3,4,8,16,128]{5,4,3,2,0,1:T(8,128)(2,1)}, bf16[3,3,4,8,16,128]{5,4,3,2,0,1:T(8,128)(2,1)S(1)}, u32[]{:S(2)}, u32[]{:S(2)}) collective-permute-start(bf16[3,3,4,8,16,128]{5,4,3,2,0,1:T(8,128)(2,1)} %get-tuple-element.7), channel_id=1, source_target_pairs={{4,0},{8,4},{12,8},{5,1},{9,5},{13,9},{6,2},{10,6},{14,10},{7,3},{... | collective-permute-start | bytes 3538952 | tf_op jit(solution)/shard_map/ppermute | solution.py:12
  125.7 50.8 %collective-permute-start.13 = (bf16[3,3,4,8,16,128]{5,4,3,2,0,1:T(8,128)(2,1)S(1)}, bf16[3,3,4,8,16,128]{5,4,3,2,0,1:T(8,128)(2,1)}, u32[]{:S(2)}, u32[]{:S(2)}) collective-permute-start(bf16[3,3,4,8,16,128]{5,4,3,2,0,1:T(8,128)(2,1)S(1)} %get-tuple-element.8), channel_id=1, source_target_pairs={{0,4},{4,8},{8,12},{1,5},{5,9},{9,13},{2,6},{6,10},{10,14},{3,7},{... | collective-permute-start | bytes 3538952 | tf_op jit(solution)/shard_map/ppermute | solution.py:12
  153.2 17.9 %copy-start.4 = (bf16[3,256,4608]{1,2,0:T(8,128)(2,1)S(1)}, bf16[3,256,4608]{1,2,0:T(8,128)(2,1)}, u32[]{:S(2)}) copy-start(bf16[3,256,4608]{1,2,0:T(8,128)(2,1)} %fusion.4) | copy-start | bytes 21233668
  164.4 21.6 %collective-permute-start.8 = (bf16[3,3,4,8,16,128]{5,4,3,2,0,1:T(8,128)(2,1)}, bf16[3,3,4,8,16,128]{5,4,3,2,0,1:T(8,128)(2,1)S(1)}, u32[]{:S(2)}, u32[]{:S(2)}) collective-permute-start(bf16[3,3,4,8,16,128]{5,4,3,2,0,1:T(8,128)(2,1)} %get-tuple-element.9), channel_id=1, source_target_pairs={{4,0},{8,4},{12,8},{5,1},{9,5},{13,9},{6,2},{10,6},{14,10},{7,3},{... | collective-permute-start | bytes 3538952 | tf_op jit(solution)/shard_map/ppermute | solution.py:12
  168.5 21.5 %collective-permute-start.9 = (bf16[3,3,4,8,16,128]{5,4,3,2,0,1:T(8,128)(2,1)S(1)}, bf16[3,3,4,8,16,128]{5,4,3,2,0,1:T(8,128)(2,1)}, u32[]{:S(2)}, u32[]{:S(2)}) collective-permute-start(bf16[3,3,4,8,16,128]{5,4,3,2,0,1:T(8,128)(2,1)S(1)} %get-tuple-element.10), channel_id=1, source_target_pairs={{0,4},{4,8},{8,12},{1,5},{5,9},{9,13},{2,6},{6,10},{10,14},{3,7},{... | collective-permute-start | bytes 3538952 | tf_op jit(solution)/shard_map/ppermute | solution.py:12
  179.3 19.9 %collective-permute-start.14 = (bf16[3,4,8,16,128]{4,3,2,1,0:T(8,128)(2,1)S(1)}, bf16[3,4,8,16,128]{4,3,2,1,0:T(8,128)(2,1)S(1)}, u32[]{:S(2)}, u32[]{:S(2)}) collective-permute-start(bf16[3,4,8,16,128]{4,3,2,1,0:T(8,128)(2,1)S(1)} %get-tuple-element.11), channel_id=1, source_target_pairs={{16,0},{17,1},{18,2},{19,3},{20,4},{21,5},{22,6},{23,7},{24,8},{25... | collective-permute-start | bytes 1179656 | tf_op jit(solution)/shard_map/ppermute | solution.py:12
  183.7 15.6 %collective-permute-start.15 = (bf16[3,4,8,16,128]{4,3,2,1,0:T(8,128)(2,1)S(1)}, bf16[3,4,8,16,128]{4,3,2,1,0:T(8,128)(2,1)S(1)}, u32[]{:S(2)}, u32[]{:S(2)}) collective-permute-start(bf16[3,4,8,16,128]{4,3,2,1,0:T(8,128)(2,1)S(1)} %get-tuple-element.12), channel_id=1, source_target_pairs={{0,16},{1,17},{2,18},{3,19},{4,20},{5,21},{6,22},{7,23},{8,24},{9,... | collective-permute-start | bytes 1179656 | tf_op jit(solution)/shard_map/ppermute | solution.py:12
  192.8 9.5 %collective-permute-start.10 = (bf16[3,4,8,16,128]{4,3,2,1,0:T(8,128)(2,1)S(1)}, bf16[3,4,8,16,128]{4,3,2,1,0:T(8,128)(2,1)S(1)}, u32[]{:S(2)}, u32[]{:S(2)}) collective-permute-start(bf16[3,4,8,16,128]{4,3,2,1,0:T(8,128)(2,1)S(1)} %get-tuple-element.13), channel_id=1, source_target_pairs={{16,0},{17,1},{18,2},{19,3},{20,4},{21,5},{22,6},{23,7},{24,8},{25... | collective-permute-start | bytes 1179656 | tf_op jit(solution)/shard_map/ppermute | solution.py:12
  197.1 9.7 %collective-permute-start.11 = (bf16[3,4,8,16,128]{4,3,2,1,0:T(8,128)(2,1)S(1)}, bf16[3,4,8,16,128]{4,3,2,1,0:T(8,128)(2,1)S(1)}, u32[]{:S(2)}, u32[]{:S(2)}) collective-permute-start(bf16[3,4,8,16,128]{4,3,2,1,0:T(8,128)(2,1)S(1)} %get-tuple-element.14), channel_id=1, source_target_pairs={{0,16},{1,17},{2,18},{3,19},{4,20},{5,21},{6,22},{7,23},{8,24},{9,... | collective-permute-start | bytes 1179656 | tf_op jit(solution)/shard_map/ppermute | solution.py:12
  (8 other events, 58.5 us)
where the time goes:
time: 208 us
  matrix products  85.6 us (41%)
  starting transfers between devices  49.4 us (24%)
  waiting for transfers between devices  32.8 us (16%)
  other arithmetic  24.4 us (12%)
  local copies, waits for them, and re-layouts  14.3 us (7%)
    ppermute x8, starting transfers between devices, shifted(): return lax.ppermute(block, axis, route)  23.8 us
    dot_general x2, matrix products, query_step(): jnp.einsum('hqk,hkd->hqd', weight_bf, v_span, preferred_element_type=jnp....  17.6 us
    dot_general x2, matrix products, query_step(): jnp.einsum('hqd,hkd->hqk', g_rows, v_span, preferred_element_type=jnp.flo...  16.9 us
    ppermute x4, starting transfers between devices, extended(): after = lax.ppermute(first, axis, down)  16.9 us
    dot_general x2, matrix products, query_step(): jnp.einsum('hqk,hqd->hkd', weight_bf, g_rows, preferred_element_type=jnp....  16.8 us
    ppermute x4, waiting for transfers between devices, extended(): before = lax.ppermute(last, axis, up)  16 us
    dot_general x2, matrix products, query_step(): jnp.einsum('hqk,hqd->hkd', d_scores, q_rows, preferred_element_type=jnp.f...  15.1 us
    dot_general x2, matrix products, scores_of(): jnp.einsum('hqd,hkd->hqk', left_rows, right_rows, preferred_element_type=...  14 us
  transfers between devices with their start and end apart: 16, of which 8 were waited for; matrix products, arithmetic and copies ran while one was open for 37% of the time, Pallas kernels for 0%

commit v1 on v0

--- a/solution.py
+++ b/solution.py
@@ -1,6 +1,10 @@
+import functools
+
 import jax
 import jax.numpy as jnp
 from jax import lax
+from jax.experimental import pallas as pl
+from jax.experimental.pallas import tpu as pltpu
 from jax.sharding import PartitionSpec as P
 
 TILE_C = 8
@@ -165,9 +169,352 @@
     return (query_grad, key_total.astype(jnp.bfloat16), value_total.astype(jnp.bfloat16))
 
 
+KEY_STEP = 256
+LOG2_E = 1.4426950408889634
+
+
+def paired_kernel(
+    q_in, k_in, v_in, g_in, q_out, k_out, v_out,
+    kb, vb, qb, gb, probs, dws, dqt, dk32, dv32, gkb, gvb, got_k, got_v, back,
+    loc, xs, xr, zs, zr, gs, gr, bs, br,
+):
+    head_count, tokens, depth = q_in.shape
+    slots = qb.shape[0]
+    queries = 2 * tokens
+    span = 2 * tokens
+    steps = span // KEY_STEP
+    scale = depth ** (-0.5)
+    x = lax.axis_index("tm")
+    z = lax.axis_index("height")
+    z_count = lax.axis_size("height")
+    parity = lax.rem(x + lax.axis_index("head"), 2)
+    other = 1 - x
+    inputs = (k_in, v_in, q_in, g_in)
+
+    def head_of(s):
+        return 2 * s + parity
+
+    def has(s, par):
+        return 2 * s + par < head_count
+
+    def live(d):
+        return (z + d - 1 >= 0) & (z + d - 1 < z_count)
+
+    barrier = pltpu.get_barrier_semaphore()
+    pl.semaphore_signal(barrier, inc=1, device_id={"tm": other})
+    for d in (0, 2):
+        @pl.when(live(d))
+        def _():
+            pl.semaphore_signal(barrier, inc=1, device_id={"height": z + d - 1})
+    pl.semaphore_wait(barrier, 1 + jnp.where(live(0), 1, 0) + jnp.where(live(2), 1, 0))
+
+    def room(a, s, f):
+        if a == 0:
+            return kb.at[s, 1, f]
+        if a == 1:
+            return vb.at[s, 1, f]
+        return (qb if a == 2 else gb).at[s, f]
+
+    def own_copy(a, s):
+        return pltpu.make_async_copy(inputs[a].at[head_of(s)], room(a, s, x), loc.at[s, a])
+
+    def swap_send(a, s):
+        return pltpu.make_async_remote_copy(
+            src_ref=inputs[a].at[2 * s + 1 - parity], dst_ref=room(a, s, x),
+            send_sem=xs.at[s, a], recv_sem=xr.at[s, a], device_id={"tm": other},
+        )
+
+    def swap_recv(a, s):
+        return pltpu.make_async_remote_copy(
+            src_ref=inputs[a].at[0], dst_ref=room(a, s, other),
+            send_sem=xs.at[s, a], recv_sem=xr.at[s, a], device_id={"tm": other},
+        )
+
+    def halo(a, s, d, mine):
+        buf = (kb, vb)[a]
+        src = inputs[a].at[head_of(s)] if mine else buf.at[s, 1, other]
+        part = 0 if mine else 1
+        return pltpu.make_async_remote_copy(
+            src_ref=src, dst_ref=buf.at[s, 2 - d, x if mine else other],
+            send_sem=zs.at[s, d, part, a], recv_sem=zr.at[s, 2 - d, part, a],
+            device_id={"height": z + d - 1},
+        )
+
+    def halo_recv(a, s, d, mine):
+        buf = (kb, vb)[a]
+        part = 0 if mine else 1
+        return pltpu.make_async_remote_copy(
+            src_ref=inputs[a].at[0], dst_ref=buf.at[s, d, x if mine else other],
+            send_sem=zs.at[s, d, part, a], recv_sem=zr.at[s, d, part, a],
+            device_id={"height": z + d - 1},
+        )
+
+    def grad_send(a, s, d):
+        return pltpu.make_async_remote_copy(
+            src_ref=(gkb, gvb)[a].at[s, d], dst_ref=(got_k, got_v)[a].at[s, 2 - d],
+            send_sem=gs.at[s, d, a], recv_sem=gr.at[s, 2 - d, a],
+            device_id={"height": z + d - 1},
+        )
+
+    def grad_recv(a, s, d):
+        return pltpu.make_async_remote_copy(
+            src_ref=(gkb, gvb)[a].at[s, d], dst_ref=(got_k, got_v)[a].at[s, d],
+            send_sem=gs.at[s, d, a], recv_sem=gr.at[s, d, a],
+            device_id={"height": z + d - 1},
+        )
+
+    def back_send(a, s):
+        return pltpu.make_async_remote_copy(
+            src_ref=back.at[s, a], dst_ref=(k_out, v_out, q_out)[a].at[head_of(s)],
+            send_sem=bs.at[s, a], recv_sem=br.at[s, a], device_id={"tm": other},
+        )
+
+    def back_recv(a, s):
+        return pltpu.make_async_remote_copy(
+            src_ref=back.at[s, a], dst_ref=(k_out, v_out, q_out)[a].at[2 * s + 1 - parity],
+            send_sem=bs.at[s, a], recv_sem=br.at[s, a], device_id={"tm": other},
+        )
+
+    for s in range(slots):
+        @pl.when(has(s, 1 - parity))
+        def _():
+            for a in range(4):
+                swap_send(a, s).start()
+
+        @pl.when(has(s, parity))
+        def _():
+            for d in (0, 2):
+                @pl.when(live(d))
+                def _():
+                    for a in range(2):
+                        halo(a, s, d, True).start()
+            for a in range(4):
+                own_copy(a, s).start()
+
+    def forward(s):
+        for a in range(2):
+            swap_recv(a, s).wait_recv()
+            for d in (0, 2):
+                @pl.when(live(d))
+                def _():
+                    halo(a, s, d, False).start()
+
+    def rows_at(d, i):
+        return pl.ds(pl.multiple_of(d * span + i * KEY_STEP, KEY_STEP), KEY_STEP)
+
+    def keys_at(ref, s, d, i):
+        per = tokens // KEY_STEP
+        return ref[s, d, i // per, pl.ds(pl.multiple_of(lax.rem(i, per) * KEY_STEP, KEY_STEP), KEY_STEP), :]
+
+    def folded(block):
+        return block.reshape(KEY_STEP // 8, 8, queries)
+
+    def score_pass(s):
+        q_rows = qb[s].reshape(queries, depth)
+
+        def over(d, top):
+            def one(i, top):
+                part = lax.dot_general(
+                    keys_at(kb, s, d, i), q_rows, (((1,), (1,)), ((), ())),
+                    preferred_element_type=jnp.float32,
+                )
+                probs[rows_at(d, i), :] = part
+                return jnp.maximum(top, jnp.max(folded(part), axis=0))
+
+            return lax.fori_loop(0, jnp.where(live(d), steps, 0), one, top)
+
+        top = over(1, jnp.full((8, queries), -jnp.inf, jnp.float32))
+        for d in (0, 2):
+            @pl.when(live(d))
+            def _():
+                for a in range(2):
+                    for mine in (True, False):
+                        halo_recv(a, s, d, mine).wait_recv()
+            top = over(d, top)
+        return jnp.max(top, axis=0, keepdims=True)
+
+    def weight_pass(s, top):
+        g_rows = gb[s].reshape(queries, depth)
+
+        def one(t, sums):
+            d, i = t // steps, lax.rem(t, steps)
+            rows = rows_at(d, i)
+            prob = jnp.exp2((probs[rows, :] - top) * (scale * LOG2_E))
+            dw = lax.dot_general(
+                keys_at(vb, s, d, i), g_rows, (((1,), (1,)), ((), ())),
+                preferred_element_type=jnp.float32,
+            )
+            probs[rows, :] = prob
+            dws[rows, :] = dw
+            return (
+                sums[0] + jnp.sum(folded(prob), axis=0),
+                sums[1] + jnp.sum(folded(prob * dw), axis=0),
+            )
+
+        zero = jnp.zeros((8, queries), jnp.float32)
+        first = jnp.where(live(0), 0, steps)
+        last = jnp.where(live(2), 3 * steps, 2 * steps)
+        total, delta = lax.fori_loop(first, last, one, (zero, zero))
+        inverse = 1.0 / jnp.sum(total, axis=0, keepdims=True)
+        return inverse, jnp.sum(delta, axis=0, keepdims=True) * inverse
+
+    def grad_pass(s, inverse, delta):
+        q_rows = qb[s].reshape(queries, depth)
+        g_rows = gb[s].reshape(queries, depth)
+        dqt[...] = jnp.zeros_like(dqt)
+
+        @pl.loop(0, 3)
+        def _(turn):
+            d = lax.rem(turn * 2, 3)
+
+            @pl.when(live(d))
+            def _():
+                @pl.loop(0, steps)
+                def _(i):
+                    rows = rows_at(d, i)
+                    weight = probs[rows, :] * inverse
+                    ds = (weight * (dws[rows, :] - delta)).astype(jnp.bfloat16)
+                    dv = jnp.dot(weight.astype(jnp.bfloat16), g_rows, preferred_element_type=jnp.float32)
+                    dk = jnp.dot(ds, q_rows, preferred_element_type=jnp.float32) * scale
+                    dqt[...] += lax.dot_general(
+                        keys_at(kb, s, d, i), ds, (((0,), (0,)), ((), ())),
+                        preferred_element_type=jnp.float32,
+                    )
+                    here = pl.ds(pl.multiple_of(i * KEY_STEP, KEY_STEP), KEY_STEP)
+                    gkb[s, d, here, :] = dk.astype(jnp.bfloat16)
+                    gvb[s, d, here, :] = dv.astype(jnp.bfloat16)
+
+                    @pl.when(d == 1)
+                    def _():
+                        dk32[s, here, :] = dk
+                        dv32[s, here, :] = dv
+
+                @pl.when(d != 1)
+                def _():
+                    for a in range(2):
+                        grad_send(a, s, d).start()
+
+        dq = (dqt[...].T * scale).astype(jnp.bfloat16).reshape(2, tokens, depth)
+
+        for f in range(2):
+            @pl.when(x == f)
+            def _():
+                q_out[head_of(s)] = dq[f]
+                back[s, 2] = dq[1 - f]
+        back_send(2, s).start()
+
+    def finish(s):
+        for a, full, got, out in ((0, dk32, got_k, k_out), (1, dv32, got_v, v_out)):
+            for d in (0, 2):
+                @pl.when(live(d))
+                def _():
+                    grad_recv(a, s, d).wait_recv()
+                    full[s] += got[s, d].astype(jnp.float32)
+            mine = pl.ds(pl.multiple_of(x * tokens, tokens), tokens)
+            theirs = pl.ds(pl.multiple_of(other * tokens, tokens), tokens)
+            back[s, a] = full[s, theirs, :].astype(jnp.bfloat16)
+            back_send(a, s).start()
+            out[head_of(s)] = full[s, mine, :].astype(jnp.bfloat16)
+
+    def ready(s):
+        for a in (2, 3):
+            swap_recv(a, s).wait_recv()
+        for a in range(4):
+            own_copy(a, s).wait()
+
+    for s in range(slots):
+        if s == 0:
+            @pl.when(has(s, parity))
+            def _():
+                forward(s)
+                ready(s)
+
+        @pl.when(has(s, parity))
+        def _():
+            top = score_pass(s)
+            if s + 1 < slots:
+                @pl.when(has(s + 1, parity))
+                def _():
+                    forward(s + 1)
+                    ready(s + 1)
+            inverse, delta = weight_pass(s, top)
+            if s > 0:
+                finish(s - 1)
+            grad_pass(s, inverse, delta)
+
+            @pl.when(jnp.logical_not(has(s + 1, parity)))
+            def _():
+                finish(s)
+
+    for s in range(slots):
+        @pl.when(has(s, 1 - parity))
+        def _():
+            for a in range(4):
+                swap_send(a, s).wait_send()
+            for a in range(3):
+                back_recv(a, s).wait_recv()
+
+        @pl.when(has(s, parity))
+        def _():
+            for d in (0, 2):
+                @pl.when(live(d))
+                def _():
+                    for a in range(2):
+                        halo(a, s, d, True).wait_send()
+                        halo(a, s, d, False).wait_send()
+                        grad_send(a, s, d).wait_send()
+            for a in range(3):
+                back_send(a, s).wait_send()
+
+
+def paired(query_in, key_in, value_in, out_grad):
+    head_count, frames, rows, cols, depth = query_in.shape
+    assert cols == 2 * TILE_C
+    tokens = frames * rows * cols
+    flat = (head_count, tokens, depth)
+    slots = (head_count + 1) // 2
+    bf, f32 = jnp.bfloat16, jnp.float32
+    dma = pltpu.SemaphoreType.DMA
+    outs = pl.pallas_call(
+        paired_kernel,
+        out_shape=[jax.ShapeDtypeStruct(flat, bf)] * 3,
+        in_specs=[pl.BlockSpec(memory_space=pltpu.VMEM)] * 4,
+        out_specs=[pl.BlockSpec(memory_space=pltpu.VMEM)] * 3,
+        scratch_shapes=[
+            pltpu.VMEM((slots, 3, 2, tokens, depth), bf),
+            pltpu.VMEM((slots, 3, 2, tokens, depth), bf),
+            pltpu.VMEM((slots, 2, tokens, depth), bf),
+            pltpu.VMEM((slots, 2, tokens, depth), bf),
+            pltpu.VMEM((6 * tokens, 2 * tokens), f32),
+            pltpu.VMEM((6 * tokens, 2 * tokens), f32),
+            pltpu.VMEM((depth, 2 * tokens), f32),
+            pltpu.VMEM((slots, 2 * tokens, depth), f32),
+            pltpu.VMEM((slots, 2 * tokens, depth), f32),
+            pltpu.VMEM((slots, 3, 2 * tokens, depth), bf),
+            pltpu.VMEM((slots, 3, 2 * tokens, depth), bf),
+            pltpu.VMEM((slots, 3, 2 * tokens, depth), bf),
+            pltpu.VMEM((slots, 3, 2 * tokens, depth), bf),
+            pltpu.VMEM((slots, 3, tokens, depth), bf),
+            dma((slots, 4)),
+            dma((slots, 4)),
+            dma((slots, 4)),
+            dma((slots, 3, 2, 2)),
+            dma((slots, 3, 2, 2)),
+            dma((slots, 3, 2)),
+            dma((slots, 3, 2)),
+            dma((slots, 3)),
+            dma((slots, 3)),
+        ],
+        compiler_params=pltpu.CompilerParams(
+            collective_id=0, has_side_effects=True, vmem_limit_bytes=60 * 1024 * 1024
+        ),
+    )(*(a.reshape(flat) for a in (query_in, key_in, value_in, out_grad)))
+    return tuple(o.reshape(query_in.shape) for o in outs)
+
+
 def solution(mesh):
     return jax.shard_map(
-        local,
+        paired if mesh.shape["tm"] == 2 else local,
         mesh=mesh,
         in_specs=(
             P("head", "tm", "height", None, None),

time: 208 us -> 62.9 us (0.30)
  the two profiles are of different devices: /device:TPU:10 before, /device:TPU:25 now
where the time goes in v1:
time: 62.9 us; the launch traced here: 62.6 us
  Pallas kernels  58.3 us (93%)
  local copies, waits for them, and re-layouts  3.7 us (6%)
  between operations  0.65 us (1%)
    pallas_call x1, Pallas kernels, paired(): pl.pallas_call(paired_kernel, out_shape=[jax.ShapeDtypeStruct(flat, bf)]...  58.3 us
    unnamed x7, local copies, waits for them, and re-layouts  3.7 us

profile of v1, /device:TPU:25, one launch (start us, length us, event | category | flops | bytes accessed | tf_op | source)
XLA Modules:
  0.0 62.6 jit_solution(567625163306609915)
XLA Ops:
  0.6 58.3 %shard_map.67 = (bf16[3,512,128]{2,1,0:T(8,128)(2,1)}, bf16[3,512,128]{2,1,0:T(8,128)(2,1)}, bf16[3,512,128]{2,1,0:T(8,128)(2,1)}) custom-call(bf16[3,512,128]{2,1,0:T(8,128)(2,1)} %bitcast.10, bf16[3,512,128]{2,1,0:T(8,128)(2,1)} %bitcast.11, bf16[3,512,128]{2,1,0:T(8,128)(2,1)} %bitcast.12, bf16[3,512,128]{2,1,0:T(8,128)(2,1)} %bitcast.13), custom_call_target="tpu_custom_call" | custom-call | tf_op jit(solution)/shard_map/pallas_call | solution.py:478
  58.9 0.0 copy-start.1
  58.9 1.8 %copy.10 = bf16[3,4,8,16,128]{4,3,2,1,0:T(8,128)(2,1)} copy(bf16[3,4,8,16,128]{4,3,2,1,0:T(8,128)(2,1)} %bitcast.9) | data formatting | bytes 786432
  60.8 0.0 copy-done.1
  60.8 0.0 copy-start
  60.8 0.7 %copy.11 = bf16[3,4,8,16,128]{4,3,2,1,0:T(8,128)(2,1)} copy(bf16[3,4,8,16,128]{4,3,2,1,0:T(8,128)(2,1)S(1)} %bitcast.8) | data formatting | bytes 786432
  61.5 0.4 copy-done
  61.9 0.7 %copy.12 = bf16[3,4,8,16,128]{4,3,2,1,0:T(8,128)(2,1)} copy(bf16[3,4,8,16,128]{4,3,2,1,0:T(8,128)(2,1)S(1)} %bitcast.7) | data formatting | bytes 786432
Async XLA Ops:
  58.9 1.8 %copy-start.1 = (bf16[3,512,128]{2,1,0:T(8,128)(2,1)S(1)}, bf16[3,512,128]{2,1,0:T(8,128)(2,1)}, u32[]{:S(2)}) copy-start(bf16[3,512,128]{2,1,0:T(8,128)(2,1)} %get-tuple-element.7) | copy-start | bytes 1179652
  60.8 1.1 %copy-start = (bf16[3,512,128]{2,1,0:T(8,128)(2,1)S(1)}, bf16[3,512,128]{2,1,0:T(8,128)(2,1)}, u32[]{:S(2)}) copy-start(bf16[3,512,128]{2,1,0:T(8,128)(2,1)} %get-tuple-element.8) | copy-start | bytes 1179652

commit v2 on v1

--- a/solution.py
+++ b/solution.py
@@ -1,5 +1,3 @@
-import functools
-
 import jax
 import jax.numpy as jnp
 from jax import lax
@@ -169,20 +167,17 @@
     return (query_grad, key_total.astype(jnp.bfloat16), value_total.astype(jnp.bfloat16))
 
 
-KEY_STEP = 256
 LOG2_E = 1.4426950408889634
 
 
 def paired_kernel(
     q_in, k_in, v_in, g_in, q_out, k_out, v_out,
-    kb, vb, qb, gb, probs, dws, dqt, dk32, dv32, gkb, gvb, got_k, got_v, back,
+    kb, vb, qb, gb, probs, dws, stats, dqt, dk32, dv32, gkb, gvb, got_k, got_v, back,
     loc, xs, xr, zs, zr, gs, gr, bs, br,
 ):
     head_count, tokens, depth = q_in.shape
     slots = qb.shape[0]
     queries = 2 * tokens
-    span = 2 * tokens
-    steps = span // KEY_STEP
     scale = depth ** (-0.5)
     x = lax.axis_index("tm")
     z = lax.axis_index("height")
@@ -240,26 +235,17 @@
             device_id={"height": z + d - 1},
         )
 
-    def halo_recv(a, s, d, mine):
-        buf = (kb, vb)[a]
-        part = 0 if mine else 1
-        return pltpu.make_async_remote_copy(
-            src_ref=inputs[a].at[0], dst_ref=buf.at[s, d, x if mine else other],
-            send_sem=zs.at[s, d, part, a], recv_sem=zr.at[s, d, part, a],
+    def grad_send(a, s, d, f, part):
+        return pltpu.make_async_remote_copy(
+            src_ref=(gkb, gvb)[a].at[s, d, f], dst_ref=(got_k, got_v)[a].at[s, 2 - d, f],
+            send_sem=gs.at[s, d, part, a], recv_sem=gr.at[s, 2 - d, part, a],
             device_id={"height": z + d - 1},
         )
 
-    def grad_send(a, s, d):
-        return pltpu.make_async_remote_copy(
-            src_ref=(gkb, gvb)[a].at[s, d], dst_ref=(got_k, got_v)[a].at[s, 2 - d],
-            send_sem=gs.at[s, d, a], recv_sem=gr.at[s, 2 - d, a],
-            device_id={"height": z + d - 1},
-        )
-
-    def grad_recv(a, s, d):
-        return pltpu.make_async_remote_copy(
-            src_ref=(gkb, gvb)[a].at[s, d], dst_ref=(got_k, got_v)[a].at[s, d],
-            send_sem=gs.at[s, d, a], recv_sem=gr.at[s, d, a],
+    def grad_recv(a, s, d, f, part):
+        return pltpu.make_async_remote_copy(
+            src_ref=(gkb, gvb)[a].at[s, d, f], dst_ref=(got_k, got_v)[a].at[s, d, f],
+            send_sem=gs.at[s, d, part, a], recv_sem=gr.at[s, d, part, a],
             device_id={"height": z + d - 1},
         )
 
@@ -275,11 +261,195 @@
             send_sem=bs.at[s, a], recv_sem=br.at[s, a], device_id={"tm": other},
         )
 
+    def for_live(d, action):
+        @pl.when(live(d))
+        def _():
+            action()
+
+    def send_own_halo(s):
+        for a in range(2):
+            for d in (0, 2):
+                for_live(d, lambda: halo(a, s, d, True).start())
+
+    def forward(s):
+        for a in range(2):
+            swap_recv(a, s).wait_recv()
+            for d in (0, 2):
+                for_live(d, lambda: halo(a, s, d, False).start())
+
+    def rows_at(d, f):
+        return pl.ds(pl.multiple_of((d * 2 + f) * tokens, tokens), tokens)
+
+    def folded(block):
+        return block.reshape(tokens // 8, 8, queries)
+
+    def arrival(turn):
+        part = turn // 3
+        return lax.rem(1 + 2 * lax.rem(turn, 3), 3), jnp.where(part == 0, x, other), part
+
+    def halo_wait(a, s, d, f, part):
+        @pl.when(d != 1)
+        def _():
+            pltpu.make_async_remote_copy(
+                src_ref=inputs[a].at[0], dst_ref=(kb, vb)[a].at[s, d, f],
+                send_sem=zs.at[s, d, part, a], recv_sem=zr.at[s, d, part, a],
+                device_id={"height": z + d - 1},
+            ).wait_recv()
+
+    def score_pass(s, half):
+        @pl.loop(3 * half, 3 * half + 3)
+        def _(turn):
+            d, f, part = arrival(turn)
+
+            @pl.when(live(d))
+            def _():
+                halo_wait(0, s, d, f, part)
+                block = lax.dot_general(
+                    kb[s, d, f], qb[s].reshape(queries, depth), (((1,), (1,)), ((), ())),
+                    preferred_element_type=jnp.float32,
+                )
+                probs[rows_at(d, f), :] = block
+                stats[0] = jnp.maximum(stats[0], jnp.max(folded(block), axis=0))
+
+    def weight_pass(s):
+        stats[1] = jnp.zeros_like(stats[1])
+        stats[2] = jnp.zeros_like(stats[2])
+        top = jnp.max(stats[0], axis=0, keepdims=True)
+
+        @pl.loop(0, 6)
+        def _(turn):
+            d, f, part = arrival(turn)
+
+            @pl.when(live(d))
+            def _():
+                halo_wait(1, s, d, f, part)
+                rows = rows_at(d, f)
+                prob = jnp.exp2((probs[rows, :] - top) * (scale * LOG2_E))
+                dw = lax.dot_general(
+                    vb[s, d, f], gb[s].reshape(queries, depth), (((1,), (1,)), ((), ())),
+                    preferred_element_type=jnp.float32,
+                )
+                probs[rows, :] = prob
+                dws[rows, :] = dw
+                stats[1] += jnp.sum(folded(prob), axis=0)
+                stats[2] += jnp.sum(folded(prob * dw), axis=0)
+
+    def grad_pass(s):
+        inverse = 1.0 / jnp.sum(stats[1], axis=0, keepdims=True)
+        delta = jnp.sum(stats[2], axis=0, keepdims=True) * inverse
+        dqt[...] = jnp.zeros_like(dqt)
+
+        @pl.loop(0, 6)
+        def _(turn):
+            d = lax.rem(2 * lax.rem(turn, 3), 3)
+            part = 1 - turn // 3
+            f = jnp.where(part == 0, x, other)
+            if s > 0:
+                @pl.when(turn == 5)
+                def _():
+                    finish(s - 1)
+
+            @pl.when(live(d))
+            def _():
+                rows = rows_at(d, f)
+                weight = probs[rows, :] * inverse
+                ds = (weight * (dws[rows, :] - delta)).astype(jnp.bfloat16)
+                dv = jnp.dot(
+                    weight.astype(jnp.bfloat16), gb[s].reshape(queries, depth),
+                    preferred_element_type=jnp.float32,
+                )
+                dk = jnp.dot(
+                    ds, qb[s].reshape(queries, depth), preferred_element_type=jnp.float32
+                ) * scale
+                dqt[...] += lax.dot_general(
+                    kb[s, d, f], ds, (((0,), (0,)), ((), ())),
+                    preferred_element_type=jnp.float32,
+                )
+
+                @pl.when(d == 1)
+                def _():
+                    dk32[s, f] = dk
+                    dv32[s, f] = dv
+
+                @pl.when(d != 1)
+                def _():
+                    gkb[s, d, f] = dk.astype(jnp.bfloat16)
+                    gvb[s, d, f] = dv.astype(jnp.bfloat16)
+                    for a in range(2):
+                        grad_send(a, s, d, f, part).start()
+
+        dq = (dqt[...].T * scale).astype(jnp.bfloat16).reshape(2, tokens, depth)
+        for f in range(2):
+            @pl.when(x == f)
+            def _():
+                back[s, 2] = dq[1 - f]
+                q_out[head_of(s)] = dq[f]
+        back_send(2, s).start()
+
+    def finish(s):
+        for part in (1, 0):
+            f = other if part else x
+            for a, full, got, out in ((0, dk32, got_k, k_out), (1, dv32, got_v, v_out)):
+                for d in (0, 2):
+                    @pl.when(live(d))
+                    def _():
+                        grad_recv(a, s, d, f, part).wait_recv()
+                        full[s, f] += got[s, d, f].astype(jnp.float32)
+                if part:
+                    back[s, a] = full[s, f].astype(jnp.bfloat16)
+                    back_send(a, s).start()
+                else:
+                    out[head_of(s)] = full[s, f].astype(jnp.bfloat16)
+
     for s in range(slots):
         @pl.when(has(s, 1 - parity))
         def _():
+            for a in (2, 0, 1, 3):
+                swap_send(a, s).start()
+
+        @pl.when(has(s, parity))
+        def _():
+            if s == 0:
+                send_own_halo(s)
+            for a in (2, 0, 1, 3):
+                own_copy(a, s).start()
+
+    for s in range(slots):
+        @pl.when(has(s, parity))
+        def _():
+            stats[0] = jnp.full_like(stats[0], -jnp.inf)
+            for a in (2, 0, 1, 3):
+                own_copy(a, s).wait()
+            swap_recv(2, s).wait_recv()
+            score_pass(s, 0)
+            if s == 0:
+                forward(s)
+                if slots > 1:
+                    @pl.when(has(1, parity))
+                    def _():
+                        send_own_halo(1)
+            score_pass(s, 1)
+            swap_recv(3, s).wait_recv()
+            weight_pass(s)
+            if s + 1 < slots:
+                @pl.when(has(s + 1, parity))
+                def _():
+                    if s > 0:
+                        send_own_halo(s + 1)
+                    forward(s + 1)
+            grad_pass(s)
+
+            @pl.when(jnp.logical_not(has(s + 1, parity)))
+            def _():
+                finish(s)
+
+    for s in range(slots):
+        @pl.when(has(s, 1 - parity))
+        def _():
             for a in range(4):
-                swap_send(a, s).start()
+                swap_send(a, s).wait_send()
+            for a in range(3):
+                back_recv(a, s).wait_recv()
 
         @pl.when(has(s, parity))
         def _():
@@ -287,182 +457,9 @@
                 @pl.when(live(d))
                 def _():
                     for a in range(2):
-                        halo(a, s, d, True).start()
-            for a in range(4):
-                own_copy(a, s).start()
-
-    def forward(s):
-        for a in range(2):
-            swap_recv(a, s).wait_recv()
-            for d in (0, 2):
-                @pl.when(live(d))
-                def _():
-                    halo(a, s, d, False).start()
-
-    def rows_at(d, i):
-        return pl.ds(pl.multiple_of(d * span + i * KEY_STEP, KEY_STEP), KEY_STEP)
-
-    def keys_at(ref, s, d, i):
-        per = tokens // KEY_STEP
-        return ref[s, d, i // per, pl.ds(pl.multiple_of(lax.rem(i, per) * KEY_STEP, KEY_STEP), KEY_STEP), :]
-
-    def folded(block):
-        return block.reshape(KEY_STEP // 8, 8, queries)
-
-    def score_pass(s):
-        q_rows = qb[s].reshape(queries, depth)
-
-        def over(d, top):
-            def one(i, top):
-                part = lax.dot_general(
-                    keys_at(kb, s, d, i), q_rows, (((1,), (1,)), ((), ())),
-                    preferred_element_type=jnp.float32,
-                )
-                probs[rows_at(d, i), :] = part
-                return jnp.maximum(top, jnp.max(folded(part), axis=0))
-
-            return lax.fori_loop(0, jnp.where(live(d), steps, 0), one, top)
-
-        top = over(1, jnp.full((8, queries), -jnp.inf, jnp.float32))
-        for d in (0, 2):
-            @pl.when(live(d))
-            def _():
-                for a in range(2):
-                    for mine in (True, False):
-                        halo_recv(a, s, d, mine).wait_recv()
-            top = over(d, top)
-        return jnp.max(top, axis=0, keepdims=True)
-
-    def weight_pass(s, top):
-        g_rows = gb[s].reshape(queries, depth)
-
-        def one(t, sums):
-            d, i = t // steps, lax.rem(t, steps)
-            rows = rows_at(d, i)
-            prob = jnp.exp2((probs[rows, :] - top) * (scale * LOG2_E))
-            dw = lax.dot_general(
-                keys_at(vb, s, d, i), g_rows, (((1,), (1,)), ((), ())),
-                preferred_element_type=jnp.float32,
-            )
-            probs[rows, :] = prob
-            dws[rows, :] = dw
-            return (
-                sums[0] + jnp.sum(folded(prob), axis=0),
-                sums[1] + jnp.sum(folded(prob * dw), axis=0),
-            )
-
-        zero = jnp.zeros((8, queries), jnp.float32)
-        first = jnp.where(live(0), 0, steps)
-        last = jnp.where(live(2), 3 * steps, 2 * steps)
-        total, delta = lax.fori_loop(first, last, one, (zero, zero))
-        inverse = 1.0 / jnp.sum(total, axis=0, keepdims=True)
-        return inverse, jnp.sum(delta, axis=0, keepdims=True) * inverse
-
-    def grad_pass(s, inverse, delta):
-        q_rows = qb[s].reshape(queries, depth)
-        g_rows = gb[s].reshape(queries, depth)
-        dqt[...] = jnp.zeros_like(dqt)
-
-        @pl.loop(0, 3)
-        def _(turn):
-            d = lax.rem(turn * 2, 3)
-
-            @pl.when(live(d))
-            def _():
-                @pl.loop(0, steps)
-                def _(i):
-                    rows = rows_at(d, i)
-                    weight = probs[rows, :] * inverse
-                    ds = (weight * (dws[rows, :] - delta)).astype(jnp.bfloat16)
-                    dv = jnp.dot(weight.astype(jnp.bfloat16), g_rows, preferred_element_type=jnp.float32)
-                    dk = jnp.dot(ds, q_rows, preferred_element_type=jnp.float32) * scale
-                    dqt[...] += lax.dot_general(
-                        keys_at(kb, s, d, i), ds, (((0,), (0,)), ((), ())),
-                        preferred_element_type=jnp.float32,
-                    )
-                    here = pl.ds(pl.multiple_of(i * KEY_STEP, KEY_STEP), KEY_STEP)
-                    gkb[s, d, here, :] = dk.astype(jnp.bfloat16)
-                    gvb[s, d, here, :] = dv.astype(jnp.bfloat16)
-
-                    @pl.when(d == 1)
-                    def _():
-                        dk32[s, here, :] = dk
-                        dv32[s, here, :] = dv
-
-                @pl.when(d != 1)
-                def _():
-                    for a in range(2):
-                        grad_send(a, s, d).start()
-
-        dq = (dqt[...].T * scale).astype(jnp.bfloat16).reshape(2, tokens, depth)
-
-        for f in range(2):
-            @pl.when(x == f)
-            def _():
-                q_out[head_of(s)] = dq[f]
-                back[s, 2] = dq[1 - f]
-        back_send(2, s).start()
-
-    def finish(s):
-        for a, full, got, out in ((0, dk32, got_k, k_out), (1, dv32, got_v, v_out)):
-            for d in (0, 2):
-                @pl.when(live(d))
-                def _():
-                    grad_recv(a, s, d).wait_recv()
-                    full[s] += got[s, d].astype(jnp.float32)
-            mine = pl.ds(pl.multiple_of(x * tokens, tokens), tokens)
-            theirs = pl.ds(pl.multiple_of(other * tokens, tokens), tokens)
-            back[s, a] = full[s, theirs, :].astype(jnp.bfloat16)
-            back_send(a, s).start()
-            out[head_of(s)] = full[s, mine, :].astype(jnp.bfloat16)
-
-    def ready(s):
-        for a in (2, 3):
-            swap_recv(a, s).wait_recv()
-        for a in range(4):
-            own_copy(a, s).wait()
-
-    for s in range(slots):
-        if s == 0:
-            @pl.when(has(s, parity))
-            def _():
-                forward(s)
-                ready(s)
-
-        @pl.when(has(s, parity))
-        def _():
-            top = score_pass(s)
-            if s + 1 < slots:
-                @pl.when(has(s + 1, parity))
-                def _():
-                    forward(s + 1)
-                    ready(s + 1)
-            inverse, delta = weight_pass(s, top)
-            if s > 0:
-                finish(s - 1)
-            grad_pass(s, inverse, delta)
-
-            @pl.when(jnp.logical_not(has(s + 1, parity)))
-            def _():
-                finish(s)
-
-    for s in range(slots):
-        @pl.when(has(s, 1 - parity))
-        def _():
-            for a in range(4):
-                swap_send(a, s).wait_send()
-            for a in range(3):
-                back_recv(a, s).wait_recv()
-
-        @pl.when(has(s, parity))
-        def _():
-            for d in (0, 2):
-                @pl.when(live(d))
-                def _():
-                    for a in range(2):
-                        halo(a, s, d, True).wait_send()
-                        halo(a, s, d, False).wait_send()
-                        grad_send(a, s, d).wait_send()
+                        for part in range(2):
+                            halo(a, s, d, part == 0).wait_send()
+                            grad_send(a, s, d, other if part else x, part).wait_send()
             for a in range(3):
                 back_send(a, s).wait_send()
 
@@ -487,21 +484,22 @@
             pltpu.VMEM((slots, 2, tokens, depth), bf),
             pltpu.VMEM((6 * tokens, 2 * tokens), f32),
             pltpu.VMEM((6 * tokens, 2 * tokens), f32),
+            pltpu.VMEM((3, 8, 2 * tokens), f32),
             pltpu.VMEM((depth, 2 * tokens), f32),
-            pltpu.VMEM((slots, 2 * tokens, depth), f32),
-            pltpu.VMEM((slots, 2 * tokens, depth), f32),
-            pltpu.VMEM((slots, 3, 2 * tokens, depth), bf),
-            pltpu.VMEM((slots, 3, 2 * tokens, depth), bf),
-            pltpu.VMEM((slots, 3, 2 * tokens, depth), bf),
-            pltpu.VMEM((slots, 3, 2 * tokens, depth), bf),
+            pltpu.VMEM((slots, 2, tokens, depth), f32),
+            pltpu.VMEM((slots, 2, tokens, depth), f32),
+            pltpu.VMEM((slots, 3, 2, tokens, depth), bf),
+            pltpu.VMEM((slots, 3, 2, tokens, depth), bf),
+            pltpu.VMEM((slots, 3, 2, tokens, depth), bf),
+            pltpu.VMEM((slots, 3, 2, tokens, depth), bf),
             pltpu.VMEM((slots, 3, tokens, depth), bf),
             dma((slots, 4)),
             dma((slots, 4)),
             dma((slots, 4)),
             dma((slots, 3, 2, 2)),
             dma((slots, 3, 2, 2)),
-            dma((slots, 3, 2)),
-            dma((slots, 3, 2)),
+            dma((slots, 3, 2, 2)),
+            dma((slots, 3, 2, 2)),
             dma((slots, 3)),
             dma((slots, 3)),
         ],

time: 62.9 us -> 53.6 us (0.85)
  the two profiles are of different devices: /device:TPU:25 before, /device:TPU:10 now
where the time goes in v2:
time: 53.6 us; the launch traced here: 53.4 us
  Pallas kernels  49 us (91%)
  local copies, waits for them, and re-layouts  3.7 us (7%)
  between operations  0.65 us (1%)
    pallas_call x1, Pallas kernels, paired(): pl.pallas_call(paired_kernel, out_shape=[jax.ShapeDtypeStruct(flat, bf)]...  49 us
    unnamed x7, local copies, waits for them, and re-layouts  3.7 us

profile of v2, /device:TPU:10, one launch (start us, length us, event | category | flops | bytes accessed | tf_op | source)
XLA Modules:
  0.0 53.4 jit_solution(16691869557098603384)
XLA Ops:
  0.6 49.0 %shard_map.67 = (bf16[3,512,128]{2,1,0:T(8,128)(2,1)}, bf16[3,512,128]{2,1,0:T(8,128)(2,1)}, bf16[3,512,128]{2,1,0:T(8,128)(2,1)}) custom-call(bf16[3,512,128]{2,1,0:T(8,128)(2,1)} %bitcast.10, bf16[3,512,128]{2,1,0:T(8,128)(2,1)} %bitcast.11, bf16[3,512,128]{2,1,0:T(8,128)(2,1)} %bitcast.12, bf16[3,512,128]{2,1,0:T(8,128)(2,1)} %bitcast.13), custom_call_target="tpu_custom_call" | custom-call | tf_op jit(solution)/shard_map/pallas_call | solution.py:475
  49.7 0.0 copy-start.1
  49.7 1.8 %copy.10 = bf16[3,4,8,16,128]{4,3,2,1,0:T(8,128)(2,1)} copy(bf16[3,4,8,16,128]{4,3,2,1,0:T(8,128)(2,1)} %bitcast.9) | data formatting | bytes 786432
  51.5 0.0 copy-done.1
  51.5 0.0 copy-start
  51.5 0.7 %copy.11 = bf16[3,4,8,16,128]{4,3,2,1,0:T(8,128)(2,1)} copy(bf16[3,4,8,16,128]{4,3,2,1,0:T(8,128)(2,1)S(1)} %bitcast.8) | data formatting | bytes 786432
  52.2 0.4 copy-done
  52.6 0.7 %copy.12 = bf16[3,4,8,16,128]{4,3,2,1,0:T(8,128)(2,1)} copy(bf16[3,4,8,16,128]{4,3,2,1,0:T(8,128)(2,1)S(1)} %bitcast.7) | data formatting | bytes 786432
Async XLA Ops:
  49.7 1.8 %copy-start.1 = (bf16[3,512,128]{2,1,0:T(8,128)(2,1)S(1)}, bf16[3,512,128]{2,1,0:T(8,128)(2,1)}, u32[]{:S(2)}) copy-start(bf16[3,512,128]{2,1,0:T(8,128)(2,1)} %get-tuple-element.7) | copy-start | bytes 1179652
  51.5 1.1 %copy-start = (bf16[3,512,128]{2,1,0:T(8,128)(2,1)S(1)}, bf16[3,512,128]{2,1,0:T(8,128)(2,1)}, u32[]{:S(2)}) copy-start(bf16[3,512,128]{2,1,0:T(8,128)(2,1)} %get-tuple-element.8) | copy-start | bytes 1179652

commit v3 on v2

--- a/solution.py
+++ b/solution.py
@@ -402,10 +402,11 @@
                     out[head_of(s)] = full[s, f].astype(jnp.bfloat16)
 
     for s in range(slots):
-        @pl.when(has(s, 1 - parity))
-        def _():
-            for a in (2, 0, 1, 3):
-                swap_send(a, s).start()
+        if s == 0:
+            @pl.when(has(s, 1 - parity))
+            def _():
+                for a in (2, 0, 1, 3):
+                    swap_send(a, s).start()
 
         @pl.when(has(s, parity))
         def _():
@@ -424,6 +425,11 @@
             score_pass(s, 0)
             if s == 0:
                 forward(s)
+                for t in range(1, slots):
+                    @pl.when(has(t, 1 - parity))
+                    def _():
+                        for a in (2, 0, 1, 3):
+                            swap_send(a, t).start()
                 if slots > 1:
                     @pl.when(has(1, parity))
                     def _():
@@ -464,6 +470,15 @@
                 back_send(a, s).wait_send()
 
 
+def settle_kernel(a_in, b_in, c_in, a_out, b_out, c_out, sems):
+    pairs = ((a_in, a_out), (b_in, b_out), (c_in, c_out))
+    copies = [pltpu.make_async_copy(src, dst, sems.at[i]) for i, (src, dst) in enumerate(pairs)]
+    for copy in copies:
+        copy.start()
+    for copy in copies:
+        copy.wait()
+
+
 def paired(query_in, key_in, value_in, out_grad):
     head_count, frames, rows, cols, depth = query_in.shape
     assert cols == 2 * TILE_C
@@ -475,7 +490,7 @@
     outs = pl.pallas_call(
         paired_kernel,
         out_shape=[jax.ShapeDtypeStruct(flat, bf)] * 3,
-        in_specs=[pl.BlockSpec(memory_space=pltpu.VMEM)] * 4,
+        in_specs=[pl.BlockSpec(memory_space=pl.ANY)] * 4,
         out_specs=[pl.BlockSpec(memory_space=pltpu.VMEM)] * 3,
         scratch_shapes=[
             pltpu.VMEM((slots, 3, 2, tokens, depth), bf),
@@ -507,6 +522,13 @@
             collective_id=0, has_side_effects=True, vmem_limit_bytes=60 * 1024 * 1024
         ),
     )(*(a.reshape(flat) for a in (query_in, key_in, value_in, out_grad)))
+    outs = pl.pallas_call(
+        settle_kernel,
+        out_shape=[jax.ShapeDtypeStruct(flat, bf)] * 3,
+        in_specs=[pl.BlockSpec(memory_space=pltpu.VMEM)] * 3,
+        out_specs=[pl.BlockSpec(memory_space=pl.ANY)] * 3,
+        scratch_shapes=[dma((3,))],
+    )(*outs)
     return tuple(o.reshape(query_in.shape) for o in outs)
 
 

time: 53.6 us -> 51 us (0.951)
  local copies, waits for them, and re-layouts: 3.7 us -> 0 us
  Pallas kernels: 49 us -> 50.2 us
    unnamed x7 -> x0, local copies, waits for them, and re-layouts: 3.7 us -> none
    pallas_call x0 -> x1, Pallas kernels: none -> 2.26 us  [paired(): pl.pallas_call(settle_kernel, out_shape=[jax.ShapeDtypeStruct(flat, bf)]...]
    pallas_call x1, Pallas kernels: 49 us -> 47.9 us  [paired(): pl.pallas_call(paired_kernel, out_shape=[jax.ShapeDtypeStruct(flat, bf)]...]
where the time goes in v3:
time: 51 us; the launch traced here: 50.8 us
  Pallas kernels  50.2 us (98%)
  between operations  0.64 us (1%)
    pallas_call x1, Pallas kernels, paired(): pl.pallas_call(paired_kernel, out_shape=[jax.ShapeDtypeStruct(flat, bf)]...  47.9 us
    pallas_call x1, Pallas kernels, paired(): pl.pallas_call(settle_kernel, out_shape=[jax.ShapeDtypeStruct(flat, bf)]...  2.26 us

profile of v3, /device:TPU:10, one launch (start us, length us, event | category | flops | bytes accessed | tf_op | source)
XLA Modules:
  0.0 50.8 jit_solution(1306319520436087609)
XLA Ops:
  0.6 47.9 %shard_map.67 = (bf16[3,512,128]{2,1,0:T(8,128)(2,1)}, bf16[3,512,128]{2,1,0:T(8,128)(2,1)}, bf16[3,512,128]{2,1,0:T(8,128)(2,1)}) custom-call(bf16[3,512,128]{2,1,0:T(8,128)(2,1)} %bitcast.7, bf16[3,512,128]{2,1,0:T(8,128)(2,1)} %bitcast.8, bf16[3,512,128]{2,1,0:T(8,128)(2,1)} %bitcast.9, bf16[3,512,128]{2,1,0:T(8,128)(2,1)} %bitcast.10), custom_call_target="tpu_custom_call" | custom-call | tf_op jit(solution)/shard_map/pallas_call | solution.py:490
  48.6 2.3 %shard_map.68 = (bf16[3,512,128]{2,1,0:T(8,128)(2,1)}, bf16[3,512,128]{2,1,0:T(8,128)(2,1)}, bf16[3,512,128]{2,1,0:T(8,128)(2,1)}) custom-call(bf16[3,512,128]{2,1,0:T(8,128)(2,1)} %get-tuple-element.9.a_in, bf16[3,512,128]{2,1,0:T(8,128)(2,1)} %get-tuple-element.10.b_in, bf16[3,512,128]{2,1,0:T(8,128)(2,1)} %get-tuple-element.11.c_in), custom_call_target="tpu_custom_call" | custom-call | tf_op jit(solution)/shard_map/pallas_call | solution.py:525

commit v4 on v3

--- a/solution.py
+++ b/solution.py
@@ -345,7 +345,7 @@
             part = 1 - turn // 3
             f = jnp.where(part == 0, x, other)
             if s > 0:
-                @pl.when(turn == 5)
+                @pl.when(turn == 3)
                 def _():
                     finish(s - 1)
 

time: 51 us -> 49.6 us (0.973)
  Pallas kernels: 50.2 us -> 48.8 us
    pallas_call x1, Pallas kernels: 47.9 us -> 46.5 us  [paired(): pl.pallas_call(paired_kernel, out_shape=[jax.ShapeDtypeStruct(flat, bf)]...]
where the time goes in v4:
time: 49.6 us; the launch traced here: 49.4 us
  Pallas kernels  48.8 us (98%)
  between operations  0.64 us (1%)
    pallas_call x1, Pallas kernels, paired(): pl.pallas_call(paired_kernel, out_shape=[jax.ShapeDtypeStruct(flat, bf)]...  46.5 us
    pallas_call x1, Pallas kernels, paired(): pl.pallas_call(settle_kernel, out_shape=[jax.ShapeDtypeStruct(flat, bf)]...  2.26 us

profile of v4, /device:TPU:10, one launch (start us, length us, event | category | flops | bytes accessed | tf_op | source)
XLA Modules:
  0.0 49.4 jit_solution(1305746127506691854)
XLA Ops:
  0.6 46.5 %shard_map.67 = (bf16[3,512,128]{2,1,0:T(8,128)(2,1)}, bf16[3,512,128]{2,1,0:T(8,128)(2,1)}, bf16[3,512,128]{2,1,0:T(8,128)(2,1)}) custom-call(bf16[3,512,128]{2,1,0:T(8,128)(2,1)} %bitcast.7, bf16[3,512,128]{2,1,0:T(8,128)(2,1)} %bitcast.8, bf16[3,512,128]{2,1,0:T(8,128)(2,1)} %bitcast.9, bf16[3,512,128]{2,1,0:T(8,128)(2,1)} %bitcast.10), custom_call_target="tpu_custom_call" | custom-call | tf_op jit(solution)/shard_map/pallas_call | solution.py:490
  47.1 2.3 %shard_map.68 = (bf16[3,512,128]{2,1,0:T(8,128)(2,1)}, bf16[3,512,128]{2,1,0:T(8,128)(2,1)}, bf16[3,512,128]{2,1,0:T(8,128)(2,1)}) custom-call(bf16[3,512,128]{2,1,0:T(8,128)(2,1)} %get-tuple-element.9.a_in, bf16[3,512,128]{2,1,0:T(8,128)(2,1)} %get-tuple-element.10.b_in, bf16[3,512,128]{2,1,0:T(8,128)(2,1)} %get-tuple-element.11.c_in), custom_call_target="tpu_custom_call" | custom-call | tf_op jit(solution)/shard_map/pallas_call | solution.py:525

commit v5 on v4

--- a/solution.py
+++ b/solution.py
@@ -470,13 +470,19 @@
                 back_send(a, s).wait_send()
 
 
-def settle_kernel(a_in, b_in, c_in, a_out, b_out, c_out, sems):
-    pairs = ((a_in, a_out), (b_in, b_out), (c_in, c_out))
-    copies = [pltpu.make_async_copy(src, dst, sems.at[i]) for i, (src, dst) in enumerate(pairs)]
-    for copy in copies:
-        copy.start()
-    for copy in copies:
-        copy.wait()
+def settle_kernel(a_in, b_in, c_in, a_out, b_out, c_out, held, sems):
+    heads = a_in.shape[0]
+    pairs = [(i, h) for h in range(heads) for i in range(3)]
+    ins, outs = (a_in, b_in, c_in), (a_out, b_out, c_out)
+    loads = [pltpu.make_async_copy(ins[i].at[h], held.at[i, h], sems.at[0, i, h]) for i, h in pairs]
+    stores = [pltpu.make_async_copy(held.at[i, h], outs[i].at[h], sems.at[1, i, h]) for i, h in pairs]
+    for load in loads:
+        load.start()
+    for load, store in zip(loads, stores):
+        load.wait()
+        store.start()
+    for store in stores:
+        store.wait()
 
 
 def paired(query_in, key_in, value_in, out_grad):
@@ -525,9 +531,9 @@
     outs = pl.pallas_call(
         settle_kernel,
         out_shape=[jax.ShapeDtypeStruct(flat, bf)] * 3,
-        in_specs=[pl.BlockSpec(memory_space=pltpu.VMEM)] * 3,
+        in_specs=[pl.BlockSpec(memory_space=pl.ANY)] * 3,
         out_specs=[pl.BlockSpec(memory_space=pl.ANY)] * 3,
-        scratch_shapes=[dma((3,))],
+        scratch_shapes=[pltpu.VMEM((3, *flat), bf), dma((2, 3, head_count))],
     )(*outs)
     return tuple(o.reshape(query_in.shape) for o in outs)
 

time: 49.6 us -> 49.4 us (level)
  no operation moved by 1% of the time
where the time goes in v5:
time: 49.4 us; the launch traced here: 49.3 us
  Pallas kernels  48.6 us (98%)
  between operations  0.64 us (1%)
    pallas_call x1, Pallas kernels, paired(): pl.pallas_call(paired_kernel, out_shape=[jax.ShapeDtypeStruct(flat, bf)]...  46.5 us
    pallas_call x1, Pallas kernels, paired(): pl.pallas_call(settle_kernel, out_shape=[jax.ShapeDtypeStruct(flat, bf)]...  2.15 us

profile of v5, /device:TPU:10, one launch (start us, length us, event | category | flops | bytes accessed | tf_op | source)
XLA Modules:
  0.0 49.3 jit_solution(11192988417121468490)
XLA Ops:
  0.6 46.5 %shard_map.67 = (bf16[3,512,128]{2,1,0:T(8,128)(2,1)}, bf16[3,512,128]{2,1,0:T(8,128)(2,1)}, bf16[3,512,128]{2,1,0:T(8,128)(2,1)}) custom-call(bf16[3,512,128]{2,1,0:T(8,128)(2,1)} %bitcast.7, bf16[3,512,128]{2,1,0:T(8,128)(2,1)} %bitcast.8, bf16[3,512,128]{2,1,0:T(8,128)(2,1)} %bitcast.9, bf16[3,512,128]{2,1,0:T(8,128)(2,1)} %bitcast.10), custom_call_target="tpu_custom_call" | custom-call | tf_op jit(solution)/shard_map/pallas_call | solution.py:496
  47.1 2.1 %shard_map.68 = (bf16[3,512,128]{2,1,0:T(8,128)(2,1)}, bf16[3,512,128]{2,1,0:T(8,128)(2,1)}, bf16[3,512,128]{2,1,0:T(8,128)(2,1)}) custom-call(bf16[3,512,128]{2,1,0:T(8,128)(2,1)} %get-tuple-element.9.a_in, bf16[3,512,128]{2,1,0:T(8,128)(2,1)} %get-tuple-element.10.b_in, bf16[3,512,128]{2,1,0:T(8,128)(2,1)} %get-tuple-element.11.c_in), custom_call_target="tpu_custom_call" | custom-call | tf_op jit(solution)/shard_map/pallas_call | solution.py:531
